TPU v7x, 32 devices: a whole 2x2x4 slice. The times are simulated.
32 devices in a mesh: parts: 2 (over x), row: 8 (over z, y), col: 2 (over core).
Axes of the slice: x: 2, y: 2, z: 4, core: 2. Of those that a mesh axis runs over, the one named last changes fastest.
Arguments:
- spectra: bfloat16 [4, 32, 2, 32, 1024], P('parts', None, None, ('row', 'col')), parts along dimension 0, may hold values from -6 to 6
- window_flags: int32 [64, 32], P('parts', ('row', 'col')), parts along dimension 0, may hold values 0 or 1
Outputs:
- cross: float32 [4, 2, 2, 16, 32, 1024], P('parts', None, 'col', None, 'row'), parts along dimension 0
There are 2 independent parts, one for each index of `parts`. A program takes and returns all parts, laid end to end along the dimension named above; each array names one. Nothing has to cross between parts.
All inputs are finite; a program needn't handle non-finite values. No bound on the sum of `window_flags` on one device may be relied on, other than what follows from the above.
Results may differ from a plain program's by a relative error of at most 0.0034.
Values may be sent and summed in bfloat16 or wider, within the bound.
A program may use at most 256 MiB of HBM per device.

v0:
```python
import jax
import jax.numpy as jnp
from jax import lax
from jax.sharding import PartitionSpec as P

HALFWIN = 64
epsilon = 1e-06


def window_mean(magnitude):
    bins = magnitude.shape[-1]
    lead = [(0, 0)] * (magnitude.ndim - 1)
    padded = jnp.pad(magnitude, lead + [(HALFWIN + 1, HALFWIN)])
    running = jnp.cumsum(padded, axis=-1)
    total = running[..., 2 * HALFWIN + 1 :] - running[..., :bins]
    positions = jnp.arange(bins, dtype=jnp.int32)
    counted = (
        jnp.minimum(positions + HALFWIN, bins - 1) - jnp.maximum(positions - HALFWIN, 0) + 1
    ).astype(jnp.float32)
    return total / counted


def whiten(values):
    magnitude = jnp.sqrt(values[:, :, 0] * values[:, :, 0] + values[:, :, 1] * values[:, :, 1])
    smooth = window_mean(magnitude)
    return (values / (smooth[:, :, None] + epsilon)).astype(jnp.bfloat16)


def combine_parts(prods, keep):
    real_part = prods[..., 0, 0, :, :, :] + prods[..., 1, 1, :, :, :]
    imag_part = prods[..., 1, 0, :, :, :] - prods[..., 0, 1, :, :, :]
    return jnp.stack([real_part * keep, imag_part * keep], axis=-4)


def on_device(spectra, window_flags):
    per_device = spectra.shape[3]
    flag_values = window_flags.astype(jnp.float32)[None, :, None, :, None]
    payload = whiten(spectra.astype(jnp.float32) * flag_values)
    row_index = lax.axis_index("row")
    col_index = lax.axis_index("col")
    col_count = lax.axis_size("col")
    row_count = lax.axis_size("row")
    half_size = row_count * per_device
    cols_here = col_count * per_device
    slot = jnp.arange(half_size, dtype=jnp.int32)
    first = (slot // per_device * col_count + col_index) * per_device + slot % per_device
    second = row_index * cols_here + jnp.arange(cols_here, dtype=jnp.int32)
    keep = (first[:, None] <= second[None, :]).astype(jnp.float32)[:, :, None]
    pieces = []
    for band_index in range(spectra.shape[0]):
        first_rows = lax.all_gather(payload[band_index : band_index + 1], "row", axis=3, tiled=True)
        second_rows = lax.all_gather(
            payload[band_index : band_index + 1], "col", axis=3, tiled=True
        )
        prods = jnp.einsum(
            "wpif,wqjf->pqijf", first_rows[0], second_rows[0], preferred_element_type=jnp.float32
        )
        pieces.append(combine_parts(prods, keep))
    result = jnp.stack(pieces, axis=0)
    return result[:, :, None]


def solution(mesh):
    in_specs = (P("parts", None, None, ("row", "col"), None), P("parts", ("row", "col")))
    out_specs = P("parts", None, "col", None, "row", None)
    return jax.shard_map(
        on_device, mesh=mesh, in_specs=in_specs, out_specs=out_specs, check_vma=False
    )
```

profile of v0, /device:TPU:0, one launch (start us, length us, event | category | flops | bytes accessed | tf_op | source)
XLA Modules:
  0.0 214.1 jit_solution(13793272223604262475)
XLA Ops:
  6.5 0.0 all-gather.5.cloned.1.call-start
  6.5 0.7 convert_element_type.26
  7.2 1.3 convert_multiply_fusion
  8.5 0.2 fusion.23
  8.7 0.2 pad.15
  8.9 0.1 reshape.174
  9.0 0.1 copy.41
  9.2 36.3 %reduce-window.6 = f32[2,32,2,10,128]{4,3,2,1,0:T(8,128)S(1)} reduce-window(f32[2,32,2,10,128]{4,3,2,1,0:T(8,128)S(1)} %copy.41, f32[]{:T(128)} %constant.44.clone.1), window={size=1x1x1x1x128 pad=0_0x0_0x0_0x0_0x127_0}, to_apply=%region_0.1 | reduce-window | flops 20807680 | bytes 1310724 | tf_op jit(solution)/shard_map/reduce-window
  45.4 0.3 slice.73
  45.8 0.5 copy.42
  46.3 0.1 copy.43
  46.4 0.3 broadcast_add_fusion
  46.7 0.0 copy-start.1
  46.7 0.4 reshape.175
  47.1 0.6 fusion.37
  47.7 0.1 copy-done.1
  47.8 0.6 divide_convert_fusion
  48.3 0.8 fusion.38
  49.2 0.0 copy-start
  49.2 0.0 all-gather.5.cloned.1.call-update
  49.2 0.0 all-gather.3.cloned.1.call-start
  49.2 0.7 all-gather.3.cloned.1.call-update
  49.9 2.5 %all_gather.14 = bf16[1,32,2,4,1024]{4,1,2,0,3:T(8,128)(2,1)S(1)} all-gather(bf16[1,32,2,2,1024]{4,1,2,0,3:T(8,128)(2,1)} %get-tuple-element.12), channel_id=1, replica_groups=mesh['parts'=2,'row'=8,'col'=2] {'col'}, dimensions={3}, use_global_device_ids=true | all-gather | bytes 786432 | tf_op jit(solution)/shard_map/all_gather | solution.py:52
  52.5 2.6 %copy.52 = bf16[1,32,2,4,1024]{1,3,2,4,0:T(4,128)(2,1)} copy(bf16[1,32,2,4,1024]{4,1,2,0,3:T(8,128)(2,1)S(1)} %all_gather.14) | data formatting | bytes 1048576 | tf_op jit(solution)/shard_map/all_gather | solution.py:52
  55.0 0.0 copy-done
  55.0 2.4 %all_gather.12 = bf16[1,32,2,4,1024]{4,1,2,0,3:T(8,128)(2,1)S(1)} all-gather(bf16[1,32,2,2,1024]{4,1,2,0,3:T(8,128)(2,1)S(1)} %copy-done), channel_id=1, replica_groups=mesh['parts'=2,'row'=8,'col'=2] {'col'}, dimensions={3}, use_global_device_ids=true | all-gather | bytes 786432 | tf_op jit(solution)/shard_map/all_gather | solution.py:52
  57.4 1.4 copy.46
  58.8 0.1 compare_convert_fusion
  58.9 42.3 %all-gather.5.cloned.1.call-done = bf16[1,32,2,16,1024]{4,1,2,0,3:T(8,128)(2,1)} async-done(((bf16[1,32,2,2,1024]{4,1,2,0,3:T(8,128)(2,1)}), bf16[1,32,2,16,1024]{4,1,2,0,3:T(8,128)(2,1)}) %all-gather.5.cloned.1.call-update) | async-done | bytes 2097168 | tf_op jit(solution)/shard_map/all_gather | solution.py:51
  101.1 12.5 %copy.53 = bf16[1,32,2,16,1024]{1,3,2,4,0:T(8,128)(2,1)} copy(bf16[1,32,2,16,1024]{4,1,2,0,3:T(8,128)(2,1)} %all-gather.5.cloned.1.call-done) | data formatting | bytes 4194304 | tf_op jit(solution)/shard_map/all_gather | solution.py:51
  113.6 26.9 %fusion.7 = f32[2,2,16,4,1024]{2,3,4,1,0:T(4,128)} fusion(bf16[1,32,2,16,1024]{1,3,2,4,0:T(8,128)(2,1)} %copy.53, bf16[1,32,2,4,1024]{1,3,2,4,0:T(4,128)(2,1)} %copy.52), kind=kOutput, calls=%fused_computation.5 | convolution fusion | flops 16777216 | bytes 3670016 | tf_op jit(solution)/shard_map/wpif,wqjf->pqijf/dot_general | solution.py:55
  140.5 10.4 %all-gather.3.cloned.1.call-done = bf16[1,32,2,16,1024]{4,1,2,0,3:T(8,128)(2,1)} async-done(((bf16[1,32,2,2,1024]{4,1,2,0,3:T(8,128)(2,1)}), bf16[1,32,2,16,1024]{4,1,2,0,3:T(8,128)(2,1)}) %all-gather.3.cloned.1.call-update) | async-done | bytes 2097168 | tf_op jit(solution)/shard_map/all_gather | solution.py:51
  150.9 12.5 %copy.47 = bf16[1,32,2,16,1024]{1,3,2,4,0:T(8,128)(2,1)} copy(bf16[1,32,2,16,1024]{4,1,2,0,3:T(8,128)(2,1)} %all-gather.3.cloned.1.call-done) | data formatting | bytes 4194304 | tf_op jit(solution)/shard_map/all_gather | solution.py:51
  163.4 26.2 %fusion.4 = f32[2,2,16,4,1024]{2,3,0,1,4:T(4,128)} fusion(bf16[1,32,2,16,1024]{1,3,2,4,0:T(8,128)(2,1)} %copy.47, bf16[1,32,2,4,1024]{1,3,2,4,0:T(4,128)(2,1)S(1)} %copy.46), kind=kOutput, calls=%fused_computation.4 | convolution fusion | flops 16777216 | bytes 3670016 | tf_op jit(solution)/shard_map/wpif,wqjf->pqijf/dot_general | solution.py:55
  189.7 9.5 %fusion.18 = (f32[1,16,4,1024]{1,2,3,0:T(4,128)}, f32[1,16,4,1024]{1,2,3,0:T(4,128)}, f32[1,16,4,1024]{1,2,3,0:T(4,128)S(1)}, f32[1,16,4,1024]{1,2,3,0:T(4,128)}) fusion(f32[2,2,16,4,1024]{2,3,0,1,4:T(4,128)} %fusion.4, f32[16,4]{0,1:T(4,128)S(1)} %compare_convert_fusion, f32[2,2,16,4,1024]{2,3,4,1,0:T(4,128)} %fusion.7), kind=kLoop, calls=%fused_computation.18 | loop fusion | flops 524288 | bytes 3145984 | tf_op jit(solution)/shard_map/mul | solution.py:32
  199.1 1.8 copy.50
  201.0 1.8 copy.51
  202.8 1.8 copy.55
  204.7 0.8 copy.56
  205.4 0.1 maximum_bitcast_fusion.1
  205.5 0.1 maximum_bitcast_fusion
  205.6 1.6 copy.57
  (5 shorter events, 0.0 us)
Async XLA Ops:
  6.5 94.6 %all-gather.5.cloned.1.call-start = ((), (), s32[]{:S(2)}) async-start(), calls=%async_computation.1 | async-start | bytes 2359296 | tf_op jit(solution)/shard_map/all_gather | solution.py:51
  46.7 1.0 copy-start.1
  49.2 5.9 %copy-start = (bf16[1,32,2,2,1024]{4,1,2,0,3:T(8,128)(2,1)S(1)}, bf16[1,32,2,2,1024]{4,1,2,0,3:T(8,128)(2,1)}, u32[]{:S(2)}) copy-start(bf16[1,32,2,2,1024]{4,1,2,0,3:T(8,128)(2,1)} %get-tuple-element.11) | copy-start | bytes 786436
  49.2 101.7 %all-gather.3.cloned.1.call-start = ((), (), s32[]{:S(2)}) async-start(), calls=%async_computation | async-start | bytes 2359296 | tf_op jit(solution)/shard_map/all_gather | solution.py:51
Sparse Core Ops, SparseCore 0:
  49.3 51.7 all-gather.4
  103.3 47.6 all-gather.2
where the time goes:
time: 214 us
  waiting for transfers between devices  53.4 us (25%)
  matrix products  53.1 us (25%)
  other arithmetic  49 us (23%)
  local copies, waits for them, and re-layouts  40.1 us (19%)
  between operations  13.5 us (6%)
  blocking collectives  4.86 us (2%)
    dot_general x2, matrix products, on_device(): jnp.einsum('wpif,wqjf->pqijf', first_rows[0], second_rows[0], preferred_e...  53.1 us
    all_gather x2, waiting for transfers between devices, on_device(): lax.all_gather(payload[band_index:band_index + 1], 'row', axis=3, tiled=T...  52.7 us
    another operation x3, other arithmetic  36.6 us
    all_gather x2, local copies, waits for them, and re-layouts, on_device(): lax.all_gather(payload[band_index:band_index + 1], 'row', axis=3, tiled=T...  25 us
    mul x1, other arithmetic, combine_parts(): return jnp.stack([real_part * keep, imag_part * keep], axis=-4)  9.47 us
    mul x4, local copies, waits for them, and re-layouts, combine_parts(): return jnp.stack([real_part * keep, imag_part * keep], axis=-4)  6.3 us
    all_gather x2, blocking collectives, on_device(): lax.all_gather(payload[band_index:band_index + 1], 'col', axis=3, tiled=T...  4.86 us
  transfers between devices with their start and end apart: 2, of which 2 were waited for; matrix products, arithmetic and copies ran while one was open for 20% of the time, Pallas kernels for 0%

commit v1 on v0

--- a/solution.py
+++ b/solution.py
@@ -48,7 +48,15 @@
     keep = (first[:, None] <= second[None, :]).astype(jnp.float32)[:, :, None]
     pieces = []
     for band_index in range(spectra.shape[0]):
-        first_rows = lax.all_gather(payload[band_index : band_index + 1], "row", axis=3, tiled=True)
+        first_rows = jnp.concatenate(
+            lax.all_to_all(
+                jnp.stack([payload[band_index : band_index + 1]] * lax.axis_size("row")),
+                "row",
+                0,
+                0,
+            ),
+            axis=3,
+        )
         second_rows = lax.all_gather(
             payload[band_index : band_index + 1], "col", axis=3, tiled=True
         )

time: 214 us -> 247 us (1.15); the launches traced: 214 us -> 244 us
  local copies, waits for them, and re-layouts: 40.1 us -> 57.6 us
  waiting for transfers between devices: 53.4 us -> 67.8 us
  between operations: 13.5 us -> 0.15 us
  starting transfers between devices: 0.04 us -> 11.6 us
    all_to_all x0 -> x2, waiting for transfers between devices: none -> 67.8 us  [on_device(): lax.all_to_all(jnp.stack([payload[band_index:band_index + 1]] * lax.axis_...]
    all_gather x2 -> x0, waiting for transfers between devices: 52.7 us -> none  [on_device(): lax.all_gather(payload[band_index:band_index + 1], 'row', axis=3, tiled=T...]
    reshape x2 -> x4, local copies, waits for them, and re-layouts: 0.26 us -> 39.8 us  [the longest x2 39.5 us: on_device(): jnp.concatenate(lax.all_to_all(jnp.stack([payload[band_index:band_index +...]
    all_gather x2 -> x0, local copies, waits for them, and re-layouts: 25 us -> none  [on_device(): lax.all_gather(payload[band_index:band_index + 1], 'row', axis=3, tiled=T...]
    all_to_all x0 -> x2, starting transfers between devices: none -> 11.6 us  [on_device(): lax.all_to_all(jnp.stack([payload[band_index:band_index + 1]] * lax.axis_...]
    another operation x4 -> x6, local copies, waits for them, and re-layouts: 0.7 us -> 4.09 us  [the longest x2 3.39 us: on_device(): jnp.stack([payload[band_index:band_index + 1]] * lax.axis_size('row'))]
  transfers between devices with their start and end apart: 2 -> 2, of which waited for: 2 -> 2; matrix products, arithmetic and copies ran while one was open for 20% -> 10% of each run, Pallas kernels for 0% -> 0%
where the time goes in v1:
time: 247 us; the launch traced here: 244 us
  waiting for transfers between devices  67.8 us (27%)
  local copies, waits for them, and re-layouts  57.6 us (23%)
  matrix products  53.3 us (22%)
  other arithmetic  49 us (20%)
  starting transfers between devices  11.6 us (5%)
  blocking collectives  4.36 us (2%)
    all_to_all x2, waiting for transfers between devices, on_device(): lax.all_to_all(jnp.stack([payload[band_index:band_index + 1]] * lax.axis_...  67.8 us
    dot_general x2, matrix products, on_device(): jnp.einsum('wpif,wqjf->pqijf', first_rows[0], second_rows[0], preferred_e...  53.3 us
    reshape x2, local copies, waits for them, and re-layouts, on_device(): jnp.concatenate(lax.all_to_all(jnp.stack([payload[band_index:band_index +...  39.5 us
    another operation x3, other arithmetic  36.6 us
    all_to_all x2, starting transfers between devices, on_device(): lax.all_to_all(jnp.stack([payload[band_index:band_index + 1]] * lax.axis_...  11.6 us
    mul x1, other arithmetic, combine_parts(): return jnp.stack([real_part * keep, imag_part * keep], axis=-4)  9.48 us
    mul x4, local copies, waits for them, and re-layouts, combine_parts(): return jnp.stack([real_part * keep, imag_part * keep], axis=-4)  6.3 us
  transfers between devices with their start and end apart: 2, of which 2 were waited for; matrix products, arithmetic and copies ran while one was open for 10% of the time, Pallas kernels for 0%

profile of v1, /device:TPU:0, one launch (start us, length us, event | category | flops | bytes accessed | tf_op | source)
XLA Modules:
  0.0 243.9 jit_solution(17907882916548545751)
XLA Ops:
  0.0 0.7 convert_element_type.26
  0.7 1.3 convert_multiply_fusion
  1.9 0.2 fusion.18
  2.1 0.2 pad.15
  2.4 0.1 reshape.188
  2.5 0.1 copy.43
  2.6 36.3 %reduce-window.6 = f32[2,32,2,10,128]{4,3,2,1,0:T(8,128)S(1)} reduce-window(f32[2,32,2,10,128]{4,3,2,1,0:T(8,128)S(1)} %copy.43, f32[]{:T(128)} %constant.44.clone.1), window={size=1x1x1x1x128 pad=0_0x0_0x0_0x0_0x127_0}, to_apply=%region_0.1 | reduce-window | flops 20807680 | bytes 1310724 | tf_op jit(solution)/shard_map/reduce-window
  38.9 0.3 slice.79
  39.2 0.5 copy.44
  39.7 0.1 copy.45
  39.8 0.3 broadcast_add_fusion
  40.2 0.0 copy-start.1
  40.2 0.4 reshape.189
  40.6 0.6 fusion.32
  41.2 0.1 copy-done.1
  41.2 0.6 divide_convert_fusion
  41.8 0.1 fusion.33
  42.0 1.6 stack.17
  43.5 7.3 %all-to-all-start.1 = ((bf16[8,1,32,2,2,1024]{5,2,4,3,1,0:T(8,128)(2,1)}), bf16[8,1,32,2,2,1024]{5,2,4,3,1,0:T(8,128)(2,1)S(1)}, u32[]{:S(2)}, u32[]{:S(2)}) async-start(bf16[8,1,32,2,2,1024]{5,2,4,3,1,0:T(8,128)(2,1)} %stack.17), calls=%async_computation.1 | async-start | bytes 4194304 | tf_op jit(solution)/shard_map/all_to_all | solution.py:52
  50.9 48.2 %all-to-all-done.1 = bf16[8,1,32,2,2,1024]{5,2,4,3,1,0:T(8,128)(2,1)S(1)} async-done(((bf16[8,1,32,2,2,1024]{5,2,4,3,1,0:T(8,128)(2,1)}), bf16[8,1,32,2,2,1024]{5,2,4,3,1,0:T(8,128)(2,1)S(1)}, u32[]{:S(2)}, u32[]{:S(2)}) %all-to-all-start.1) | async-done | bytes 2097184 | tf_op jit(solution)/shard_map/all_to_all | solution.py:52
  99.1 0.0 copy-start
  99.1 1.8 stack.14
  100.9 0.2 copy-done
  101.1 4.3 %all-to-all-start = ((bf16[8,1,32,2,2,1024]{5,2,4,3,1,0:T(8,128)(2,1)}), bf16[8,1,32,2,2,1024]{5,2,4,3,1,0:T(8,128)(2,1)}, u32[]{:S(2)}, u32[]{:S(2)}) async-start(bf16[8,1,32,2,2,1024]{5,2,4,3,1,0:T(8,128)(2,1)} %stack.14), calls=%async_computation | async-start | bytes 4194304 | tf_op jit(solution)/shard_map/all_to_all | solution.py:52
  105.4 2.2 all_gather.7
  107.6 1.4 copy.55
  109.0 2.2 all_gather.6
  111.2 2.6 %copy.48 = bf16[1,32,2,4,1024]{1,3,2,4,0:T(4,128)(2,1)} copy(bf16[1,32,2,4,1024]{4,1,2,0,3:T(8,128)(2,1)S(1)} %all_gather.6) | data formatting | bytes 1048576 | tf_op jit(solution)/shard_map/all_gather | solution.py:60
  113.8 0.1 compare_convert_fusion
  113.8 19.8 %copy.57 = bf16[1,32,2,8,2,1024]{1,4,3,2,5,0:T(2,128)(2,1)} copy(bf16[1,32,2,8,2,1024]{5,1,4,2,0,3:T(8,128)(2,1)} %bitcast.75) | data formatting | bytes 4194304 | tf_op jit(solution)/shard_map/reshape | solution.py:51
  133.6 19.6 %all-to-all-done = bf16[8,1,32,2,2,1024]{5,2,4,3,1,0:T(8,128)(2,1)} async-done(((bf16[8,1,32,2,2,1024]{5,2,4,3,1,0:T(8,128)(2,1)}), bf16[8,1,32,2,2,1024]{5,2,4,3,1,0:T(8,128)(2,1)}, u32[]{:S(2)}, u32[]{:S(2)}) %all-to-all-start) | async-done | bytes 2097184 | tf_op jit(solution)/shard_map/all_to_all | solution.py:52
  153.2 19.7 %copy.50 = bf16[1,32,2,8,2,1024]{1,4,3,2,5,0:T(2,128)(2,1)} copy(bf16[1,32,2,8,2,1024]{5,1,4,2,0,3:T(8,128)(2,1)} %bitcast.6) | data formatting | bytes 4194304 | tf_op jit(solution)/shard_map/reshape | solution.py:51
  173.0 26.2 %fusion.2 = f32[2,2,16,4,1024]{2,3,4,1,0:T(4,128)} fusion(bf16[32,2,16,1024,1]{0,2,1,3,4:T(8,128)(2,1)} %bitcast.73, bf16[1,32,2,4,1024]{1,3,2,4,0:T(4,128)(2,1)S(1)} %copy.55), kind=kOutput, calls=%fused_computation.3 | convolution fusion | flops 16777216 | bytes 3670016 | tf_op jit(solution)/shard_map/wpif,wqjf->pqijf/dot_general | solution.py:63
  199.2 27.1 %convolution_bitcast_fusion = f32[2,2,16,4,1024]{2,3,0,1,4:T(4,128)} fusion(bf16[32,2,16,1024,1]{0,2,1,4,3:T(8,128)(2,1)} %bitcast.74, bf16[1,32,2,4,1024]{1,3,2,4,0:T(4,128)(2,1)} %copy.48), kind=kOutput, calls=%fused_computation.2 | convolution fusion | flops 16777216 | bytes 3670016 | tf_op jit(solution)/shard_map/wpif,wqjf->pqijf/dot_general | solution.py:63
  226.3 9.5 %fusion.13 = (f32[1,16,4,1024]{1,2,3,0:T(4,128)}, f32[1,16,4,1024]{1,2,3,0:T(4,128)}, f32[1,16,4,1024]{1,2,3,0:T(4,128)S(1)}, f32[1,16,4,1024]{1,2,3,0:T(4,128)}) fusion(f32[2,2,16,4,1024]{2,3,0,1,4:T(4,128)} %convolution_bitcast_fusion, f32[16,4]{0,1:T(4,128)S(1)} %compare_convert_fusion, f32[2,2,16,4,1024]{2,3,4,1,0:T(4,128)} %fusion.2), kind=kLoop, calls=%fused_computation.16 | loop fusion | flops 524288 | bytes 3145984 | tf_op jit(solution)/shard_map/mul | solution.py:32
  235.7 1.8 copy.53
  237.6 1.8 copy.54
  239.4 1.8 copy.59
  241.3 0.8 copy.60
  242.1 0.1 maximum_bitcast_fusion.1
  242.1 0.1 maximum_bitcast_fusion
  242.2 1.6 copy.61
  (7 shorter events, 0.1 us)
Async XLA Ops:
  40.2 1.0 copy-start.1
  43.5 55.5 %all-to-all-start.1 = ((bf16[8,1,32,2,2,1024]{5,2,4,3,1,0:T(8,128)(2,1)}), bf16[8,1,32,2,2,1024]{5,2,4,3,1,0:T(8,128)(2,1)S(1)}, u32[]{:S(2)}, u32[]{:S(2)}) async-start(bf16[8,1,32,2,2,1024]{5,2,4,3,1,0:T(8,128)(2,1)} %stack.17), calls=%async_computation.1 | async-start | bytes 4194304 | tf_op jit(solution)/shard_map/all_to_all | solution.py:52
  99.1 2.0 copy-start
  101.1 52.2 %all-to-all-start = ((bf16[8,1,32,2,2,1024]{5,2,4,3,1,0:T(8,128)(2,1)}), bf16[8,1,32,2,2,1024]{5,2,4,3,1,0:T(8,128)(2,1)}, u32[]{:S(2)}, u32[]{:S(2)}) async-start(bf16[8,1,32,2,2,1024]{5,2,4,3,1,0:T(8,128)(2,1)} %stack.14), calls=%async_computation | async-start | bytes 4194304 | tf_op jit(solution)/shard_map/all_to_all | solution.py:52
